TPU v7x, 32 devices: a whole 2x2x4 slice. The times are simulated.
32 devices in a mesh: groups: 2 (over y), inst: 4 (over z), space: 4 (over x, core).
Axes of the slice: x: 2, y: 2, z: 4, core: 2. Of those that a mesh axis runs over, the one named last changes fastest.
Arguments:
- flow_state: float32 [8, 5, 16, 16, 128], P(('groups', 'inst'), None, 'space'), parts along dimension 0, may hold values from -1 to 1
- period_match: int32 [16], replicated, may hold values from 0 to 15, each once
Outputs:
- residual: float32 [8, 5, 16, 16, 128], P(('groups', 'inst'), None, 'space'), parts along dimension 0
There are 2 independent parts, one for each index of `groups`. A program takes and returns all parts, laid end to end along the dimension named above; an argument that names none is the same for every part. Nothing has to cross between parts.
Inputs may be any that keep to these rules, and one draw needn't show every extreme that they name: period_match is a permutation of the 16 spanwise layers.
All inputs are finite; a program needn't handle non-finite values.
Results may differ from a plain program's by a relative error of at most 0.0003.
Values sent between devices are 32-bit elements; how exact they have to be, the bound alone decides.
No kernel may reach another device: no remote copies, remote signals or barrier semaphores. Data moves between devices by JAX's collectives and lax.ppermute only.
A program may use at most 64 MiB of HBM per device.

v0:
```python
import math
import jax
import jax.numpy as jnp
from jax import lax
from jax.sharding import PartitionSpec as P

gamma_gas = 1.4
prandtl = 0.72
viscosity = 0.1
pseudo_step = 0.03
entropy_share = 0.1


def from_behind(block, axis, distance):
    devices = range(lax.axis_size(axis))
    route = [((i - distance) % len(devices), i) for i in devices]
    return lax.ppermute(block, axis, route)


def extended(cells, sides, width):
    for axis, dim in sides:
        count = lax.axis_size(axis)
        ends = count - 1
        head = lax.slice_in_dim(cells, 0, width, axis=dim)
        tail = lax.slice_in_dim(cells, cells.shape[dim] - width, cells.shape[dim], axis=dim)
        cells = jnp.concatenate(
            [
                lax.ppermute(tail, axis, [(i, (i + 1) % count) for i in range(ends)]),
                cells,
                lax.ppermute(head, axis, [((i + 1) % count, i) for i in range(ends)]),
            ],
            axis=dim,
        )
    return cells


def from_draw(draws):
    shape = (5,) + (1,) * (draws.ndim - 1)
    offsets = jnp.array([1.0, 0.8, 0.0, 0.0, 0.8], jnp.float32).reshape(shape)
    spreads = jnp.array([0.3, 0.3, 0.3, 0.3, 0.2], jnp.float32).reshape(shape)
    return offsets + spreads * draws


def conserved(primitives):
    dens = primitives[0]
    velocity = primitives[1:4]
    kinetic = 0.5 * dens * jnp.sum(velocity * velocity, axis=0)
    energy = primitives[4] / (gamma_gas - 1.0) + kinetic
    return jnp.concatenate([dens[None], dens[None] * velocity, energy[None]], axis=0)


def primitive(conserved_vars):
    dens = conserved_vars[0]
    velocity = conserved_vars[1:4] / dens
    pressure = (gamma_gas - 1.0) * (
        conserved_vars[4] - 0.5 * dens * jnp.sum(velocity * velocity, axis=0)
    )
    return jnp.concatenate([dens[None], velocity, pressure[None]], axis=0)


def entropy_fix(eigen_val, sound_speed):
    spread = entropy_share * sound_speed
    magnitude = jnp.abs(eigen_val)
    return jnp.where(
        magnitude >= spread, magnitude, (eigen_val * eigen_val + spread * spread) / (2.0 * spread)
    )


def euler_flux(dens, velocity, pressure, enthalpy, normal):
    normal_vel = velocity[normal]
    values = [dens * normal_vel]
    for component in range(3):
        moment = dens * velocity[component] * normal_vel
        if component == normal:
            moment = moment + pressure
        values.append(moment)
    values.append(dens * enthalpy * normal_vel)
    return values


def face_flux(left_cells, right_cells, normal):
    dens_left, vel_left, pres_left = (left_cells[0], left_cells[1:4], left_cells[4])
    dens_right, vel_right, pres_right = (right_cells[0], right_cells[1:4], right_cells[4])
    ratio = gamma_gas / (gamma_gas - 1.0)
    sq_left = jnp.sum(vel_left * vel_left, axis=0)
    sq_right = jnp.sum(vel_right * vel_right, axis=0)
    enth_left = ratio * pres_left / dens_left + 0.5 * sq_left
    enth_right = ratio * pres_right / dens_right + 0.5 * sq_right
    flux_left = euler_flux(dens_left, vel_left, pres_left, enth_left, normal)
    flux_right = euler_flux(dens_right, vel_right, pres_right, enth_right, normal)
    root_left = jnp.sqrt(dens_left)
    root_right = jnp.sqrt(dens_right)
    root_sum = root_left + root_right
    vel_roe = (root_left * vel_left + root_right * vel_right) / root_sum
    enth_roe = (root_left * enth_left + root_right * enth_right) / root_sum
    speed_sq = jnp.sum(vel_roe * vel_roe, axis=0)
    sound_sq = (gamma_gas - 1.0) * (enth_roe - 0.5 * speed_sq)
    sound_speed = jnp.sqrt(sound_sq)
    normal_vel = vel_roe[normal]
    dens_roe = root_left * root_right
    jump_dens = dens_right - dens_left
    jump_pres = pres_right - pres_left
    jump_vel = vel_right - vel_left
    jump_normal = jump_vel[normal]
    wave_slow = (jump_pres - dens_roe * sound_speed * jump_normal) / (2.0 * sound_sq)
    wave_fast = (jump_pres + dens_roe * sound_speed * jump_normal) / (2.0 * sound_sq)
    wave_mid = jump_dens - jump_pres / sound_sq
    eigen_mid = entropy_fix(normal_vel, sound_speed)
    flux_slow = entropy_fix(normal_vel - sound_speed, sound_speed) * wave_slow
    flux_fast = entropy_fix(normal_vel + sound_speed, sound_speed) * wave_fast
    dissipation = [flux_slow + eigen_mid * wave_mid + flux_fast]
    for component in range(3):
        unit_dir = 1.0 if component == normal else 0.0
        term = flux_slow * (vel_roe[component] - unit_dir * sound_speed)
        term = term + eigen_mid * (
            wave_mid * vel_roe[component]
            + dens_roe * (jump_vel[component] - unit_dir * jump_normal)
        )
        term = term + flux_fast * (vel_roe[component] + unit_dir * sound_speed)
        dissipation.append(term)
    shear_work = jnp.sum(vel_roe * jump_vel, axis=0) - normal_vel * jump_normal
    energy_term = flux_slow * (enth_roe - normal_vel * sound_speed)
    energy_term = energy_term + eigen_mid * (wave_mid * 0.5 * speed_sq + dens_roe * shear_work)
    energy_term = energy_term + flux_fast * (enth_roe + normal_vel * sound_speed)
    dissipation.append(energy_term)
    jump_temp = pres_right / dens_right - pres_left / dens_left
    jump_kin = 0.5 * (sq_right - sq_left)
    viscous_terms = [
        jnp.zeros_like(jump_dens),
        jump_vel[0],
        jump_vel[1],
        jump_vel[2],
        jump_kin + gamma_gas / ((gamma_gas - 1.0) * prandtl) * jump_temp,
    ]
    values = []
    for component in range(5):
        values.append(
            0.5 * (flux_left[component] + flux_right[component])
            - 0.5 * dissipation[component]
            - viscosity * viscous_terms[component]
        )
    return jnp.stack(values, axis=0)


def flux_change(padded, along, normal):
    length = padded.shape[along]
    face_values = face_flux(
        lax.slice_in_dim(padded, 0, length - 1, axis=along),
        lax.slice_in_dim(padded, 1, length, axis=along),
        normal,
    )
    return lax.slice_in_dim(face_values, 1, length - 1, axis=along) - lax.slice_in_dim(
        face_values, 0, length - 2, axis=along
    )


def spectral_entry(offset, number):
    wrapped = jnp.mod(offset, number)
    parity = 1.0 - 2.0 * jnp.mod(wrapped, 2).astype(jnp.float32)
    angles = math.pi * wrapped.astype(jnp.float32) / number
    sine_val = jnp.where(wrapped == 0, 1.0, jnp.sin(angles))
    derivative = jnp.where(
        wrapped == 0, 0.0, math.pi / number * parity * jnp.cos(angles) / sine_val
    )
    return derivative + 0.5 * parity


def on_device(flow_state, period_match):
    instances = lax.axis_size("inst")
    phase_lag = instances // 4
    instance = lax.axis_index("inst")
    space_parts = lax.axis_size("space")
    position = lax.axis_index("space")
    labels = jnp.arange(period_match.shape[0], dtype=jnp.int32)
    matches = (period_match[:, None] == labels[None, :]).astype(jnp.int32)
    inverse = jnp.sum(labels[:, None] * matches, axis=0)
    mirror = jnp.array([1.0, 1.0, 1.0, -1.0, 1.0], jnp.float32).reshape(5, 1, 1, 1)

    def lagged(plane, steps):
        return from_behind(plane, "inst", steps)

    def timewise(conserved_vars):
        pieces = lax.all_gather(conserved_vars[None], "inst", axis=0, tiled=True)
        number = pieces.shape[0]
        others = jnp.arange(number, dtype=jnp.int32)
        weights = spectral_entry(instance - others, instances)
        return jnp.tensordot(weights, pieces, axes=1, precision=lax.Precision.HIGHEST)

    def evaluate(conserved_vars):
        prims = primitive(conserved_vars)
        padded = extended(prims, (("space", 1),), 1)
        lower_edge = jnp.where(position == 0, prims[:, :1], padded[:, :1])
        upper_edge = jnp.where(position == space_parts - 1, prims[:, -1:], padded[:, -1:])
        along_axial = jnp.concatenate([lower_edge, prims, upper_edge], axis=1)
        along_span = jnp.concatenate(
            [prims[:, :, :1] * mirror, prims, prims[:, :, -1:] * mirror], axis=2
        )
        ghost_below = jnp.take(lagged(prims[..., -1], phase_lag), period_match, axis=2)
        ghost_above = jnp.take(lagged(prims[..., 0], -phase_lag), inverse, axis=2)
        along_pitch = jnp.concatenate(
            [ghost_below[..., None], prims, ghost_above[..., None]], axis=3
        )
        spatial = (
            flux_change(along_axial, 1, 0)
            + flux_change(along_span, 2, 2)
            + flux_change(along_pitch, 3, 1)
        )
        return timewise(conserved_vars) + spatial

    initial = conserved(from_draw(flow_state[0]))
    section_state = initial - pseudo_step * evaluate(initial)
    return evaluate(section_state)[None]


def solution(mesh):
    in_specs = (P(("groups", "inst"), None, "space", None, None), P())
    out_specs = P(("groups", "inst"), None, "space", None, None)
    return jax.shard_map(
        on_device, mesh=mesh, in_specs=in_specs, out_specs=out_specs, check_vma=False
    )
```

profile of v0, /device:TPU:1, one launch (start us, length us, event | category | flops | bytes accessed | tf_op | source)
XLA Modules:
  0.0 72.5 jit_solution(7410314620236597218)
XLA Ops:
  0.0 0.7 copy-done.1
  0.7 1.0 %fusion.15 = f32[5,4,16,128]{3,2,1,0:T(8,128)S(1)} fusion(f32[1,5,4,16,128]{4,3,2,1,0:T(8,128)} %param.7, f32[5]{0:T(128)S(1)} %copy-done.1, f32[5]{0:T(128)S(1)} %copy-done.2), kind=kLoop, calls=%fused_computation.59 | loop fusion | flops 81920 | bytes 327720 | tf_op jit(solution)/shard_map/add | solution.py:41
  1.9 0.5 copy.46
  2.4 2.2 %collective-permute-start.2 = (f32[5,4,16]{0,1,2:T(4,128)S(1)}, f32[5,4,16]{0,1,2:T(4,128)S(1)}, u32[]{:S(2)}, u32[]{:S(2)}) collective-permute-start(f32[5,4,16]{0,1,2:T(4,128)S(1)} %bitcast.389), channel_id=1, source_target_pairs={{12,0},{0,4},{4,8},{8,12},{13,1},{1,5},{5,9},{9,13},{14,2},{2,6},{... | collective-permute-start | bytes 3848 | tf_op jit(solution)/shard_map/ppermute | solution.py:17
  4.5 0.5 copy.49
  5.0 2.1 %collective-permute-start.3 = (f32[5,4,16]{0,1,2:T(4,128)S(1)}, f32[5,4,16]{0,1,2:T(4,128)S(1)}, u32[]{:S(2)}, u32[]{:S(2)}) collective-permute-start(f32[5,4,16]{0,1,2:T(4,128)S(1)} %bitcast.388), channel_id=1, source_target_pairs={{4,0},{8,4},{12,8},{0,12},{5,1},{9,5},{13,9},{1,13},{6,2},{10,6},{... | collective-permute-start | bytes 3848 | tf_op jit(solution)/shard_map/ppermute | solution.py:17
  7.1 4.2 %collective-permute-start = (f32[5,1,16,128]{3,2,1,0:T(8,128)S(1)}, f32[5,1,16,128]{3,2,1,0:T(8,128)S(1)}, u32[]{:S(2)}, u32[]{:S(2)}) collective-permute-start(f32[5,1,16,128]{3,2,1,0:T(8,128)S(1)} %get-tuple-element.119), channel_id=1, source_target_pairs={{0,1},{1,2},{2,3},{4,5},{5,6},{6,7},{8,9},{9,10},{10,11},{12,13},{... | collective-permute-start | bytes 122888 | tf_op jit(solution)/shard_map/ppermute | solution.py:28
  11.3 1.9 %collective-permute-start.1 = (f32[5,1,16,128]{3,2,1,0:T(8,128)S(1)}, f32[5,1,16,128]{3,2,1,0:T(8,128)S(1)}, u32[]{:S(2)}, u32[]{:S(2)}) collective-permute-start(f32[5,1,16,128]{3,2,1,0:T(8,128)S(1)} %get-tuple-element.120), channel_id=1, source_target_pairs={{1,0},{2,1},{3,2},{5,4},{6,5},{7,6},{9,8},{10,9},{11,10},{13,12},{... | collective-permute-start | bytes 122888 | tf_op jit(solution)/shard_map/ppermute | solution.py:30
  13.4 13.8 %all-gather = f32[20,4,16,128]{3,2,1,0:T(8,128)S(1)} all-gather(f32[5,4,16,128]{3,2,1,0:T(8,128)S(1)} %get-tuple-element.130), channel_id=2, replica_groups=mesh['groups'=2,'inst'=4,'space'=4] {'inst'}, dimensions={0}, use_global_device_ids=true | all-gather | bytes 819200 | tf_op jit(solution)/shard_map/all_gather | solution.py:183
  27.2 0.6 copy-done
  28.6 1.5 %fusion.2 = f32[1,5,4,16,128]{4,0,3,2,1:T(1,128)S(1)} fusion(f32[4,5,4,16,128]{4,3,2,1,0:T(8,128)S(1)} %bitcast.384, s32[]{:T(128)S(6)} %axis_index.23), kind=kOutput, calls=%fused_computation.6 | convolution fusion | flops 1966224 | bytes 819204 | tf_op jit(solution)/shard_map/dot_general | solution.py:187
  30.3 0.6 gather_fusion
  31.0 0.6 copy.31
  31.6 0.6 gather_fusion.1
  32.3 0.6 copy.34
  32.8 0.2 maximum_maximum_fusion
  33.2 0.2 subtract_dynamic-update-slice_fusion.3
  33.8 0.2 fusion.61
  34.9 14.5 %all-gather.1 = f32[20,4,16,128]{3,2,1,0:T(8,128)S(1)} all-gather(f32[5,4,16,128]{3,2,1,0:T(8,128)S(1)} %fusion.13), channel_id=3, replica_groups=mesh['groups'=2,'inst'=4,'space'=4] {'inst'}, dimensions={0}, use_global_device_ids=true | all-gather | bytes 819200 | tf_op jit(solution)/shard_map/all_gather | solution.py:183
  49.6 1.5 %fusion = f32[1,5,4,16,128]{4,0,3,2,1:T(1,128)S(1)} fusion(f32[4,5,4,16,128]{4,3,2,1,0:T(8,128)S(1)} %bitcast.385, s32[]{:T(128)S(6)} %axis_index.23), kind=kOutput, calls=%fused_computation.4 | convolution fusion | flops 1966224 | bytes 819204 | tf_op jit(solution)/shard_map/dot_general | solution.py:187
  51.2 0.5 copy.52
  51.7 0.5 copy.53
  52.2 3.3 %collective-permute-start.7 = (f32[5,4,16]{0,1,2:T(4,128)S(1)}, f32[5,4,16]{0,1,2:T(4,128)S(1)}, u32[]{:S(2)}, u32[]{:S(2)}) collective-permute-start(f32[5,4,16]{0,1,2:T(4,128)S(1)} %bitcast.390), channel_id=1, source_target_pairs={{4,0},{8,4},{12,8},{0,12},{5,1},{9,5},{13,9},{1,13},{6,2},{10,6},{... | collective-permute-start | bytes 3848 | tf_op jit(solution)/shard_map/ppermute | solution.py:17
  56.1 8.9 %collective-permute-start.4 = (f32[5,1,16,128]{3,2,1,0:T(8,128)S(1)}, f32[5,1,16,128]{3,2,1,0:T(8,128)S(1)}, u32[]{:S(2)}, u32[]{:S(2)}) collective-permute-start(f32[5,1,16,128]{3,2,1,0:T(8,128)S(1)} %get-tuple-element.105), channel_id=1, source_target_pairs={{0,1},{1,2},{2,3},{4,5},{5,6},{6,7},{8,9},{9,10},{10,11},{12,13},{... | collective-permute-start | bytes 122888 | tf_op jit(solution)/shard_map/ppermute | solution.py:28
  65.0 2.1 %collective-permute-start.5 = (f32[5,1,16,128]{3,2,1,0:T(8,128)S(1)}, f32[5,1,16,128]{3,2,1,0:T(8,128)S(1)}, u32[]{:S(2)}, u32[]{:S(2)}) collective-permute-start(f32[5,1,16,128]{3,2,1,0:T(8,128)S(1)} %get-tuple-element.106), channel_id=1, source_target_pairs={{1,0},{2,1},{3,2},{5,4},{6,5},{7,6},{9,8},{10,9},{11,10},{13,12},{... | collective-permute-start | bytes 122888 | tf_op jit(solution)/shard_map/ppermute | solution.py:30
  67.3 0.6 gather_fusion.2
  68.0 0.6 copy.36
  68.5 0.6 gather_fusion.3
  69.2 0.6 copy.39
  70.1 0.2 subtract_dynamic-update-slice_fusion.1
  70.8 0.2 fusion.50
  71.7 0.8 %fusion.8 = f32[1,5,4,16,128]{4,3,2,1,0:T(8,128)} fusion(f32[5,4,16,128]{3,2,1,0:T(8,128)S(1)} %bitcast.386, f32[5,4,16,129]{3,2,1,0:T(8,128)S(1)} %fusion.50, f32[5,4,17,128]{3,2,1,0:T(8,128)S(1)} %constant_dynamic-update-slice_fusion.15, f32[5,5,16,128]{3,2,1,0:T(8,128)S(1)} %constant_dynamic-update-slice_fusion.10), kind=kLoop, calls=%fused_computation.45 | loop fusion | flops 245760 | bytes 1310720 | tf_op jit(solution)/shard_map/broadcast_in_dim | solution.py:212
  (86 shorter events, 5.4 us)
Async XLA Ops:
  0.0 0.7 copy-start.1
  0.0 0.7 copy-start.2
  2.4 27.9 %collective-permute-start.2 = (f32[5,4,16]{0,1,2:T(4,128)S(1)}, f32[5,4,16]{0,1,2:T(4,128)S(1)}, u32[]{:S(2)}, u32[]{:S(2)}) collective-permute-start(f32[5,4,16]{0,1,2:T(4,128)S(1)} %bitcast.389), channel_id=1, source_target_pairs={{12,0},{0,4},{4,8},{8,12},{13,1},{1,5},{5,9},{9,13},{14,2},{2,6},{... | collective-permute-start | bytes 3848 | tf_op jit(solution)/shard_map/ppermute | solution.py:17
  5.0 26.5 %collective-permute-start.3 = (f32[5,4,16]{0,1,2:T(4,128)S(1)}, f32[5,4,16]{0,1,2:T(4,128)S(1)}, u32[]{:S(2)}, u32[]{:S(2)}) collective-permute-start(f32[5,4,16]{0,1,2:T(4,128)S(1)} %bitcast.388), channel_id=1, source_target_pairs={{4,0},{8,4},{12,8},{0,12},{5,1},{9,5},{13,9},{1,13},{6,2},{10,6},{... | collective-permute-start | bytes 3848 | tf_op jit(solution)/shard_map/ppermute | solution.py:17
  7.1 26.9 %collective-permute-start = (f32[5,1,16,128]{3,2,1,0:T(8,128)S(1)}, f32[5,1,16,128]{3,2,1,0:T(8,128)S(1)}, u32[]{:S(2)}, u32[]{:S(2)}) collective-permute-start(f32[5,1,16,128]{3,2,1,0:T(8,128)S(1)} %get-tuple-element.119), channel_id=1, source_target_pairs={{0,1},{1,2},{2,3},{4,5},{5,6},{6,7},{8,9},{9,10},{10,11},{12,13},{... | collective-permute-start | bytes 122888 | tf_op jit(solution)/shard_map/ppermute | solution.py:28
  11.3 1.9 %copy-start.3 = (s32[16]{0:T(128)S(1)}, s32[16]{0:T(128)}, u32[]{:S(2)}) copy-start(s32[16]{0:T(128)} %param.8) | copy-start | bytes 196
  11.3 22.7 %collective-permute-start.1 = (f32[5,1,16,128]{3,2,1,0:T(8,128)S(1)}, f32[5,1,16,128]{3,2,1,0:T(8,128)S(1)}, u32[]{:S(2)}, u32[]{:S(2)}) collective-permute-start(f32[5,1,16,128]{3,2,1,0:T(8,128)S(1)} %get-tuple-element.120), channel_id=1, source_target_pairs={{1,0},{2,1},{3,2},{5,4},{6,5},{7,6},{9,8},{10,9},{11,10},{13,12},{... | collective-permute-start | bytes 122888 | tf_op jit(solution)/shard_map/ppermute | solution.py:30
  27.2 0.7 copy-start
  51.7 15.6 %collective-permute-start.6 = (f32[5,4,16]{0,1,2:T(4,128)S(1)}, f32[5,4,16]{0,1,2:T(4,128)S(1)}, u32[]{:S(2)}, u32[]{:S(2)}) collective-permute-start(f32[5,4,16]{0,1,2:T(4,128)S(1)} %bitcast.391), channel_id=1, source_target_pairs={{12,0},{0,4},{4,8},{8,12},{13,1},{1,5},{5,9},{9,13},{14,2},{2,6},{... | collective-permute-start | bytes 3848 | tf_op jit(solution)/shard_map/ppermute | solution.py:17
  52.2 16.3 %collective-permute-start.7 = (f32[5,4,16]{0,1,2:T(4,128)S(1)}, f32[5,4,16]{0,1,2:T(4,128)S(1)}, u32[]{:S(2)}, u32[]{:S(2)}) collective-permute-start(f32[5,4,16]{0,1,2:T(4,128)S(1)} %bitcast.390), channel_id=1, source_target_pairs={{4,0},{8,4},{12,8},{0,12},{5,1},{9,5},{13,9},{1,13},{6,2},{10,6},{... | collective-permute-start | bytes 3848 | tf_op jit(solution)/shard_map/ppermute | solution.py:17
  56.1 14.8 %collective-permute-start.4 = (f32[5,1,16,128]{3,2,1,0:T(8,128)S(1)}, f32[5,1,16,128]{3,2,1,0:T(8,128)S(1)}, u32[]{:S(2)}, u32[]{:S(2)}) collective-permute-start(f32[5,1,16,128]{3,2,1,0:T(8,128)S(1)} %get-tuple-element.105), channel_id=1, source_target_pairs={{0,1},{1,2},{2,3},{4,5},{5,6},{6,7},{8,9},{9,10},{10,11},{12,13},{... | collective-permute-start | bytes 122888 | tf_op jit(solution)/shard_map/ppermute | solution.py:28
  65.0 5.9 %collective-permute-start.5 = (f32[5,1,16,128]{3,2,1,0:T(8,128)S(1)}, f32[5,1,16,128]{3,2,1,0:T(8,128)S(1)}, u32[]{:S(2)}, u32[]{:S(2)}) collective-permute-start(f32[5,1,16,128]{3,2,1,0:T(8,128)S(1)} %get-tuple-element.106), channel_id=1, source_target_pairs={{1,0},{2,1},{3,2},{5,4},{6,5},{7,6},{9,8},{10,9},{11,10},{13,12},{... | collective-permute-start | bytes 122888 | tf_op jit(solution)/shard_map/ppermute | solution.py:30
where the time goes:
time: 72.7 us; the launch traced here: 72.5 us
  blocking collectives  28.3 us (39%)
  starting transfers between devices  24.6 us (34%)
  local copies, waits for them, and re-layouts  8.14 us (11%)
  other arithmetic  7.8 us (11%)
  matrix products  3.1 us (4%)
    all_gather x2, blocking collectives, timewise(): pieces = lax.all_gather(conserved_vars[None], 'inst', axis=0, tiled=True)  28.3 us
    ppermute x2, starting transfers between devices, extended(): lax.ppermute(tail, axis, [(i, (i + 1) % count) for i in range(ends)])  13 us
    ppermute x4, starting transfers between devices, from_behind(): return lax.ppermute(block, axis, route)  7.53 us
    ppermute x2, starting transfers between devices, extended(): lax.ppermute(head, axis, [((i + 1) % count, i) for i in range(ends)])  4.02 us
    dot_general x2, matrix products, timewise(): jnp.tensordot(weights, pieces, axes=1, precision=lax.Precision.HIGHEST)  3.1 us
    unnamed x24, other arithmetic  3.02 us
  transfers between devices with their start and end apart: 8, of which 0 were waited for; matrix products, arithmetic and copies ran while one was open for 16% of the time, Pallas kernels for 0%

commit v1 on v0

--- a/solution.py
+++ b/solution.py
@@ -180,7 +180,17 @@
         return from_behind(plane, "inst", steps)
 
     def timewise(conserved_vars):
-        pieces = lax.all_gather(conserved_vars[None], "inst", axis=0, tiled=True)
+        piece_in = conserved_vars[None]
+        frames = [piece_in]
+        dev_count = lax.axis_size("inst")
+        for src_i in range(dev_count - 1):
+            after = lax.ppermute(
+                frames[-1], "inst", perm=[(p, (p + 1) % dev_count) for p in range(dev_count)]
+            )
+            frames.append(after)
+        w2 = jnp.concatenate(frames[::-1], 0)
+        piece_out = lax.axis_index("inst")
+        pieces = jnp.roll(w2, (piece_out + 1) * piece_in.shape[0], 0)
         number = pieces.shape[0]
         others = jnp.arange(number, dtype=jnp.int32)
         weights = spectral_entry(instance - others, instances)

time: 72.7 us -> 68 us (0.935)
  blocking collectives: 28.3 us -> 0 us
  waiting for transfers between devices: 0.02 us -> 25.1 us
  starting transfers between devices: 24.6 us -> 22.8 us
  local copies, waits for them, and re-layouts: 8.14 us -> 6.83 us
  other arithmetic: 7.8 us -> 8.55 us
    all_gather x2 -> x0, blocking collectives: 28.3 us -> none  [timewise(): pieces = lax.all_gather(conserved_vars[None], 'inst', axis=0, tiled=True)]
    ppermute x0 -> x6, waiting for transfers between devices: none -> 25.1 us  [timewise(): lax.ppermute(frames[-1], 'inst', perm=[(p, (p + 1) % dev_count) for p in...]
    ppermute x2, starting transfers between devices: 13 us -> 9.98 us  [extended(): lax.ppermute(tail, axis, [(i, (i + 1) % count) for i in range(ends)])]
    ppermute x0 -> x6, starting transfers between devices: none -> 2.36 us  [timewise(): lax.ppermute(frames[-1], 'inst', perm=[(p, (p + 1) % dev_count) for p in...]
    unnamed x8 -> x4, local copies, waits for them, and re-layouts: 1.32 us -> 0.01 us
    ppermute x4, starting transfers between devices: 7.53 us -> 6.62 us  [from_behind(): return lax.ppermute(block, axis, route)]
    concatenate x0 -> x2, other arithmetic: none -> 0.75 us  [timewise(): pieces = jnp.roll(w2, (piece_out + 1) * piece_in.shape[0], 0)]
  transfers between devices with their start and end apart: 8 -> 14, of which waited for: 0 -> 4; matrix products, arithmetic and copies ran while one was open for 16% -> 18% of each run, Pallas kernels for 0% -> 0%
where the time goes in v1:
time: 68 us; the launch traced here: 67.1 us
  waiting for transfers between devices  25.1 us (37%)
  starting transfers between devices  22.8 us (34%)
  other arithmetic  8.55 us (13%)
  local copies, waits for them, and re-layouts  6.83 us (10%)
  matrix products  3.1 us (5%)
    ppermute x6, waiting for transfers between devices, timewise(): lax.ppermute(frames[-1], 'inst', perm=[(p, (p + 1) % dev_count) for p in...  25.1 us
    ppermute x2, starting transfers between devices, extended(): lax.ppermute(tail, axis, [(i, (i + 1) % count) for i in range(ends)])  9.98 us
    ppermute x4, starting transfers between devices, from_behind(): return lax.ppermute(block, axis, route)  6.62 us
    ppermute x2, starting transfers between devices, extended(): lax.ppermute(head, axis, [((i + 1) % count, i) for i in range(ends)])  3.84 us
    dot_general x2, matrix products, timewise(): jnp.tensordot(weights, pieces, axes=1, precision=lax.Precision.HIGHEST)  3.1 us
    unnamed x24, other arithmetic  3.01 us
    ppermute x6, starting transfers between devices, timewise(): lax.ppermute(frames[-1], 'inst', perm=[(p, (p + 1) % dev_count) for p in...  2.36 us
  transfers between devices with their start and end apart: 14, of which 4 were waited for; matrix products, arithmetic and copies ran while one was open for 18% of the time, Pallas kernels for 0%

profile of v1, /device:TPU:1, one launch (start us, length us, event | category | flops | bytes accessed | tf_op | source)
XLA Modules:
  0.0 67.1 jit_solution(5233077839174097120)
XLA Ops:
  0.0 1.0 %fusion.29 = f32[5,4,16,128]{3,2,1,0:T(8,128)S(1)} fusion(f32[1,5,4,16,128]{4,3,2,1,0:T(8,128)} %param.9, f32[5]{0:T(128)} %constant.139.clone, f32[5]{0:T(128)} %constant.138.clone), kind=kLoop, calls=%fused_computation.89 | loop fusion | flops 81920 | bytes 327720 | tf_op jit(solution)/shard_map/add | solution.py:41
  1.2 2.2 %collective-permute-start = (f32[1,5,4,16,128]{4,3,2,1,0:T(8,128)S(1)}, f32[1,5,4,16,128]{4,3,2,1,0:T(8,128)S(1)}, u32[]{:S(2)}, u32[]{:S(2)}) collective-permute-start(f32[1,5,4,16,128]{4,3,2,1,0:T(8,128)S(1)} %get-tuple-element.132), channel_id=1, source_target_pairs={{0,4},{4,8},{8,12},{12,0},{1,5},{5,9},{9,13},{13,1},{2,6},{6,10},{... | collective-permute-start | bytes 491528 | tf_op jit(solution)/shard_map/ppermute | solution.py:187
  3.4 0.5 copy.35
  3.9 1.3 %collective-permute-start.5 = (f32[5,4,16]{0,1,2:T(4,128)S(1)}, f32[5,4,16]{0,1,2:T(4,128)S(1)}, u32[]{:S(2)}, u32[]{:S(2)}) collective-permute-start(f32[5,4,16]{0,1,2:T(4,128)S(1)} %bitcast.390), channel_id=1, source_target_pairs={{12,0},{0,4},{4,8},{8,12},{13,1},{1,5},{5,9},{9,13},{14,2},{2,6},{... | collective-permute-start | bytes 3848 | tf_op jit(solution)/shard_map/ppermute | solution.py:17
  5.3 0.5 copy.38
  5.8 2.0 %collective-permute-start.6 = (f32[5,4,16]{0,1,2:T(4,128)S(1)}, f32[5,4,16]{0,1,2:T(4,128)S(1)}, u32[]{:S(2)}, u32[]{:S(2)}) collective-permute-start(f32[5,4,16]{0,1,2:T(4,128)S(1)} %bitcast.389), channel_id=1, source_target_pairs={{4,0},{8,4},{12,8},{0,12},{5,1},{9,5},{13,9},{1,13},{6,2},{10,6},{... | collective-permute-start | bytes 3848 | tf_op jit(solution)/shard_map/ppermute | solution.py:17
  7.8 4.5 %collective-permute-start.3 = (f32[5,1,16,128]{3,2,1,0:T(8,128)S(1)}, f32[5,1,16,128]{3,2,1,0:T(8,128)S(1)}, u32[]{:S(2)}, u32[]{:S(2)}) collective-permute-start(f32[5,1,16,128]{3,2,1,0:T(8,128)S(1)} %get-tuple-element.120), channel_id=1, source_target_pairs={{0,1},{1,2},{2,3},{4,5},{5,6},{6,7},{8,9},{9,10},{10,11},{12,13},{... | collective-permute-start | bytes 122888 | tf_op jit(solution)/shard_map/ppermute | solution.py:28
  12.3 1.9 %collective-permute-start.4 = (f32[5,1,16,128]{3,2,1,0:T(8,128)S(1)}, f32[5,1,16,128]{3,2,1,0:T(8,128)S(1)}, u32[]{:S(2)}, u32[]{:S(2)}) collective-permute-start(f32[5,1,16,128]{3,2,1,0:T(8,128)S(1)} %get-tuple-element.121), channel_id=1, source_target_pairs={{1,0},{2,1},{3,2},{5,4},{6,5},{7,6},{9,8},{10,9},{11,10},{13,12},{... | collective-permute-start | bytes 122888 | tf_op jit(solution)/shard_map/ppermute | solution.py:30
  15.3 0.6 gather_fusion
  16.0 0.6 copy.20
  16.6 0.6 gather_fusion.1
  17.2 0.6 copy.23
  18.2 0.2 subtract_dynamic-update-slice_fusion.3
  19.7 5.9 %collective-permute-done.1 = f32[1,5,4,16,128]{4,3,2,1,0:T(8,128)S(1)} collective-permute-done((f32[1,5,4,16,128]{4,3,2,1,0:T(8,128)S(1)}, f32[1,5,4,16,128]{4,3,2,1,0:T(8,128)S(1)}, u32[]{:S(2)}, u32[]{:S(2)}) %collective-permute-start.1) | collective-permute-done | bytes 163872 | tf_op jit(solution)/shard_map/ppermute | solution.py:187
  25.6 6.9 %collective-permute-done.2 = f32[1,5,4,16,128]{4,3,2,1,0:T(8,128)S(1)} collective-permute-done((f32[1,5,4,16,128]{4,3,2,1,0:T(8,128)S(1)}, f32[1,5,4,16,128]{4,3,2,1,0:T(8,128)S(1)}, u32[]{:S(2)}, u32[]{:S(2)}) %collective-permute-start.2) | collective-permute-done | bytes 163872 | tf_op jit(solution)/shard_map/ppermute | solution.py:187
  32.5 0.4 fusion.10
  32.9 1.5 %fusion.16 = f32[1,5,4,16,128]{4,0,3,2,1:T(1,128)S(1)} fusion(f32[4,5,4,16,128]{4,3,2,1,0:T(8,128)S(1)} %fusion.10, s32[]{:T(128)S(6)} %axis_index.15), kind=kOutput, calls=%fused_computation.36 | convolution fusion | flops 1966224 | bytes 819204 | tf_op jit(solution)/shard_map/dot_general | solution.py:197
  34.9 0.5 copy.41
  35.5 0.5 copy.42
  36.0 3.3 %collective-permute-start.13 = (f32[5,4,16]{0,1,2:T(4,128)S(1)}, f32[5,4,16]{0,1,2:T(4,128)S(1)}, u32[]{:S(2)}, u32[]{:S(2)}) collective-permute-start(f32[5,4,16]{0,1,2:T(4,128)S(1)} %bitcast.391), channel_id=1, source_target_pairs={{4,0},{8,4},{12,8},{0,12},{5,1},{9,5},{13,9},{1,13},{6,2},{10,6},{... | collective-permute-start | bytes 3848 | tf_op jit(solution)/shard_map/ppermute | solution.py:17
  39.9 5.5 %collective-permute-start.10 = (f32[5,1,16,128]{3,2,1,0:T(8,128)S(1)}, f32[5,1,16,128]{3,2,1,0:T(8,128)S(1)}, u32[]{:S(2)}, u32[]{:S(2)}) collective-permute-start(f32[5,1,16,128]{3,2,1,0:T(8,128)S(1)} %get-tuple-element.106), channel_id=1, source_target_pairs={{0,1},{1,2},{2,3},{4,5},{5,6},{6,7},{8,9},{9,10},{10,11},{12,13},{... | collective-permute-start | bytes 122888 | tf_op jit(solution)/shard_map/ppermute | solution.py:28
  45.4 1.9 %collective-permute-start.11 = (f32[5,1,16,128]{3,2,1,0:T(8,128)S(1)}, f32[5,1,16,128]{3,2,1,0:T(8,128)S(1)}, u32[]{:S(2)}, u32[]{:S(2)}) collective-permute-start(f32[5,1,16,128]{3,2,1,0:T(8,128)S(1)} %get-tuple-element.107), channel_id=1, source_target_pairs={{1,0},{2,1},{3,2},{5,4},{6,5},{7,6},{9,8},{10,9},{11,10},{13,12},{... | collective-permute-start | bytes 122888 | tf_op jit(solution)/shard_map/ppermute | solution.py:30
  47.5 0.6 gather_fusion.2
  48.1 0.6 copy.25
  48.7 0.6 gather_fusion.3
  49.4 0.6 copy.28
  50.3 0.2 subtract_dynamic-update-slice_fusion.1
  51.8 5.9 %collective-permute-done.8 = f32[1,5,4,16,128]{4,3,2,1,0:T(8,128)S(1)} collective-permute-done((f32[1,5,4,16,128]{4,3,2,1,0:T(8,128)S(1)}, f32[1,5,4,16,128]{4,3,2,1,0:T(8,128)S(1)}, u32[]{:S(2)}, u32[]{:S(2)}) %collective-permute-start.8) | collective-permute-done | bytes 163872 | tf_op jit(solution)/shard_map/ppermute | solution.py:187
  57.8 6.5 %collective-permute-done.9 = f32[1,5,4,16,128]{4,3,2,1,0:T(8,128)S(1)} collective-permute-done((f32[1,5,4,16,128]{4,3,2,1,0:T(8,128)S(1)}, f32[1,5,4,16,128]{4,3,2,1,0:T(8,128)S(1)}, u32[]{:S(2)}, u32[]{:S(2)}) %collective-permute-start.9) | collective-permute-done | bytes 163872 | tf_op jit(solution)/shard_map/ppermute | solution.py:187
  64.3 0.4 fusion.3
  64.7 1.5 %fusion.14 = f32[1,5,4,16,128]{4,0,3,2,1:T(1,128)S(1)} fusion(f32[4,5,4,16,128]{4,3,2,1,0:T(8,128)S(1)} %fusion.3, s32[]{:T(128)S(6)} %axis_index.15), kind=kOutput, calls=%fused_computation.34 | convolution fusion | flops 1966224 | bytes 819204 | tf_op jit(solution)/shard_map/dot_general | solution.py:197
  66.3 0.8 %fusion.22 = f32[1,5,4,16,128]{4,3,2,1,0:T(8,128)} fusion(f32[5,4,16,128]{3,2,1,0:T(8,128)S(1)} %bitcast.387, f32[5,4,16,129]{3,2,1,0:T(8,128)S(1)} %fusion.65, f32[5,4,17,128]{3,2,1,0:T(8,128)S(1)} %constant_dynamic-update-slice_fusion.15, f32[5,5,16,128]{3,2,1,0:T(8,128)S(1)} %constant_dynamic-update-slice_fusion.10), kind=kLoop, calls=%fused_computation.75 | loop fusion | flops 245760 | bytes 1310720 | tf_op jit(solution)/shard_map/broadcast_in_dim | solution.py:222
  (94 shorter events, 6.1 us)
Async XLA Ops:
  1.1 13.1 %copy-start.1 = (s32[16]{0:T(128)S(1)}, s32[16]{0:T(128)}, u32[]{:S(2)}) copy-start(s32[16]{0:T(128)} %param.10) | copy-start | bytes 196
  1.1 13.2 %copy-start = (f32[5]{0:T(128)S(1)}, f32[5]{0:T(128)}, u32[]{:S(2)}) copy-start(f32[5]{0:T(128)} %constant.137.clone) | copy-start | bytes 64
  1.2 18.3 %collective-permute-start = (f32[1,5,4,16,128]{4,3,2,1,0:T(8,128)S(1)}, f32[1,5,4,16,128]{4,3,2,1,0:T(8,128)S(1)}, u32[]{:S(2)}, u32[]{:S(2)}) collective-permute-start(f32[1,5,4,16,128]{4,3,2,1,0:T(8,128)S(1)} %get-tuple-element.132), channel_id=1, source_target_pairs={{0,4},{4,8},{8,12},{12,0},{1,5},{5,9},{9,13},{13,1},{2,6},{6,10},{... | collective-permute-start | bytes 491528 | tf_op jit(solution)/shard_map/ppermute | solution.py:187
  3.9 11.4 %collective-permute-start.5 = (f32[5,4,16]{0,1,2:T(4,128)S(1)}, f32[5,4,16]{0,1,2:T(4,128)S(1)}, u32[]{:S(2)}, u32[]{:S(2)}) collective-permute-start(f32[5,4,16]{0,1,2:T(4,128)S(1)} %bitcast.390), channel_id=1, source_target_pairs={{12,0},{0,4},{4,8},{8,12},{13,1},{1,5},{5,9},{9,13},{14,2},{2,6},{... | collective-permute-start | bytes 3848 | tf_op jit(solution)/shard_map/ppermute | solution.py:17
  5.8 10.8 %collective-permute-start.6 = (f32[5,4,16]{0,1,2:T(4,128)S(1)}, f32[5,4,16]{0,1,2:T(4,128)S(1)}, u32[]{:S(2)}, u32[]{:S(2)}) collective-permute-start(f32[5,4,16]{0,1,2:T(4,128)S(1)} %bitcast.389), channel_id=1, source_target_pairs={{4,0},{8,4},{12,8},{0,12},{5,1},{9,5},{13,9},{1,13},{6,2},{10,6},{... | collective-permute-start | bytes 3848 | tf_op jit(solution)/shard_map/ppermute | solution.py:17
  7.8 11.2 %collective-permute-start.3 = (f32[5,1,16,128]{3,2,1,0:T(8,128)S(1)}, f32[5,1,16,128]{3,2,1,0:T(8,128)S(1)}, u32[]{:S(2)}, u32[]{:S(2)}) collective-permute-start(f32[5,1,16,128]{3,2,1,0:T(8,128)S(1)} %get-tuple-element.120), channel_id=1, source_target_pairs={{0,1},{1,2},{2,3},{4,5},{5,6},{6,7},{8,9},{9,10},{10,11},{12,13},{... | collective-permute-start | bytes 122888 | tf_op jit(solution)/shard_map/ppermute | solution.py:28
  12.3 6.7 %collective-permute-start.4 = (f32[5,1,16,128]{3,2,1,0:T(8,128)S(1)}, f32[5,1,16,128]{3,2,1,0:T(8,128)S(1)}, u32[]{:S(2)}, u32[]{:S(2)}) collective-permute-start(f32[5,1,16,128]{3,2,1,0:T(8,128)S(1)} %get-tuple-element.121), channel_id=1, source_target_pairs={{1,0},{2,1},{3,2},{5,4},{6,5},{7,6},{9,8},{10,9},{11,10},{13,12},{... | collective-permute-start | bytes 122888 | tf_op jit(solution)/shard_map/ppermute | solution.py:30
  19.5 6.0 %collective-permute-start.1 = (f32[1,5,4,16,128]{4,3,2,1,0:T(8,128)S(1)}, f32[1,5,4,16,128]{4,3,2,1,0:T(8,128)S(1)}, u32[]{:S(2)}, u32[]{:S(2)}) collective-permute-start(f32[1,5,4,16,128]{4,3,2,1,0:T(8,128)S(1)} %collective-permute-done), channel_id=1, source_target_pairs={{0,4},{4,8},{8,12},{12,0},{1,5},{5,9},{9,13},{13,1},{2,6},{6,10},{... | collective-permute-start | bytes 491528 | tf_op jit(solution)/shard_map/ppermute | solution.py:187
  25.5 7.0 %collective-permute-start.2 = (f32[1,5,4,16,128]{4,3,2,1,0:T(8,128)S(1)}, f32[1,5,4,16,128]{4,3,2,1,0:T(8,128)S(1)}, u32[]{:S(2)}, u32[]{:S(2)}) collective-permute-start(f32[1,5,4,16,128]{4,3,2,1,0:T(8,128)S(1)} %collective-permute-done.1), channel_id=1, source_target_pairs={{0,4},{4,8},{8,12},{12,0},{1,5},{5,9},{9,13},{13,1},{2,6},{6,10},{... | collective-permute-start | bytes 491528 | tf_op jit(solution)/shard_map/ppermute | solution.py:187
  34.9 16.8 %collective-permute-start.7 = (f32[1,5,4,16,128]{4,3,2,1,0:T(8,128)S(1)}, f32[1,5,4,16,128]{4,3,2,1,0:T(8,128)S(1)}, u32[]{:S(2)}, u32[]{:S(2)}) collective-permute-start(f32[1,5,4,16,128]{4,3,2,1,0:T(8,128)S(1)} %bitcast.385), channel_id=1, source_target_pairs={{0,4},{4,8},{8,12},{12,0},{1,5},{5,9},{9,13},{13,1},{2,6},{6,10},{... | collective-permute-start | bytes 491528 | tf_op jit(solution)/shard_map/ppermute | solution.py:187
  35.4 12.0 %collective-permute-start.12 = (f32[5,4,16]{0,1,2:T(4,128)S(1)}, f32[5,4,16]{0,1,2:T(4,128)S(1)}, u32[]{:S(2)}, u32[]{:S(2)}) collective-permute-start(f32[5,4,16]{0,1,2:T(4,128)S(1)} %bitcast.392), channel_id=1, source_target_pairs={{12,0},{0,4},{4,8},{8,12},{13,1},{1,5},{5,9},{9,13},{14,2},{2,6},{... | collective-permute-start | bytes 3848 | tf_op jit(solution)/shard_map/ppermute | solution.py:17
  36.0 12.7 %collective-permute-start.13 = (f32[5,4,16]{0,1,2:T(4,128)S(1)}, f32[5,4,16]{0,1,2:T(4,128)S(1)}, u32[]{:S(2)}, u32[]{:S(2)}) collective-permute-start(f32[5,4,16]{0,1,2:T(4,128)S(1)} %bitcast.391), channel_id=1, source_target_pairs={{4,0},{8,4},{12,8},{0,12},{5,1},{9,5},{13,9},{1,13},{6,2},{10,6},{... | collective-permute-start | bytes 3848 | tf_op jit(solution)/shard_map/ppermute | solution.py:17
  39.9 11.2 %collective-permute-start.10 = (f32[5,1,16,128]{3,2,1,0:T(8,128)S(1)}, f32[5,1,16,128]{3,2,1,0:T(8,128)S(1)}, u32[]{:S(2)}, u32[]{:S(2)}) collective-permute-start(f32[5,1,16,128]{3,2,1,0:T(8,128)S(1)} %get-tuple-element.106), channel_id=1, source_target_pairs={{0,1},{1,2},{2,3},{4,5},{5,6},{6,7},{8,9},{9,10},{10,11},{12,13},{... | collective-permute-start | bytes 122888 | tf_op jit(solution)/shard_map/ppermute | solution.py:28
  45.4 5.8 %collective-permute-start.11 = (f32[5,1,16,128]{3,2,1,0:T(8,128)S(1)}, f32[5,1,16,128]{3,2,1,0:T(8,128)S(1)}, u32[]{:S(2)}, u32[]{:S(2)}) collective-permute-start(f32[5,1,16,128]{3,2,1,0:T(8,128)S(1)} %get-tuple-element.107), channel_id=1, source_target_pairs={{1,0},{2,1},{3,2},{5,4},{6,5},{7,6},{9,8},{10,9},{11,10},{13,12},{... | collective-permute-start | bytes 122888 | tf_op jit(solution)/shard_map/ppermute | solution.py:30
  51.7 6.0 %collective-permute-start.8 = (f32[1,5,4,16,128]{4,3,2,1,0:T(8,128)S(1)}, f32[1,5,4,16,128]{4,3,2,1,0:T(8,128)S(1)}, u32[]{:S(2)}, u32[]{:S(2)}) collective-permute-start(f32[1,5,4,16,128]{4,3,2,1,0:T(8,128)S(1)} %collective-permute-done.7), channel_id=1, source_target_pairs={{0,4},{4,8},{8,12},{12,0},{1,5},{5,9},{9,13},{13,1},{2,6},{6,10},{... | collective-permute-start | bytes 491528 | tf_op jit(solution)/shard_map/ppermute | solution.py:187
  57.7 6.7 %collective-permute-start.9 = (f32[1,5,4,16,128]{4,3,2,1,0:T(8,128)S(1)}, f32[1,5,4,16,128]{4,3,2,1,0:T(8,128)S(1)}, u32[]{:S(2)}, u32[]{:S(2)}) collective-permute-start(f32[1,5,4,16,128]{4,3,2,1,0:T(8,128)S(1)} %collective-permute-done.8), channel_id=1, source_target_pairs={{0,4},{4,8},{8,12},{12,0},{1,5},{5,9},{9,13},{13,1},{2,6},{6,10},{... | collective-permute-start | bytes 491528 | tf_op jit(solution)/shard_map/ppermute | solution.py:187
